TPU v7x, 32 devices: a whole 2x2x4 slice. The times are simulated.
32 devices in a mesh: grp: 1, col: 32 (over z, y, x, core).
Axes of the slice: x: 2, y: 2, z: 4, core: 2. Of those that a mesh axis runs over, the one named last changes fastest.
Arguments:
- pair: bfloat16 [16, 1024, 128], P('grp', 'col'), may hold values from -6 to 6
- w_query: bfloat16 [128, 128], replicated, may hold values from -0.5 to 0.5
- w_kv: bfloat16 [128, 256], replicated, may hold values from -0.5 to 0.5
- w_gate: bfloat16 [128, 128], replicated, may hold values from -0.5 to 0.5
- w_out: bfloat16 [128, 128], replicated, may hold values from -0.5 to 0.5
- pair_bias: bfloat16 [4, 1024, 1024], P('grp', 'col'), may hold values from -8 to 300
- lengths: int32 [1], P('grp'), may hold values from 512 to 1024
Outputs:
- update: bfloat16 [16, 1024, 128], P('grp', 'col')
All inputs are finite; a program needn't handle non-finite values.
Results may differ from a plain program's by a relative error of at most 0.0081.
Values may be sent and summed in bfloat16 or wider, within the bound.
No kernel may reach another device: no remote copies, remote signals or barrier semaphores. Data moves between devices by JAX's collectives and lax.ppermute only.
A program may use at most 128 MiB of HBM per device.

v0:
```python
import jax
import jax.numpy as jnp
from jax import lax
from jax.sharding import PartitionSpec as P

HEADS = 4


def normalize(pair_block):
    values_f = pair_block.astype(jnp.float32)
    mean_val = jnp.mean(values_f, axis=-1, keepdims=True)
    centred = values_f - mean_val
    variance = jnp.mean(centred * centred, axis=-1, keepdims=True)
    return (centred * lax.rsqrt(variance + 1e-05)).astype(jnp.bfloat16)


def attend(normed, bias_query, key_limit, w_query, w_kv, w_gate, w_out, gather_keys):
    row_count, col_count, chan_count = normed.shape
    head_width = chan_count // HEADS
    queries = (
        jnp.dot(normed, w_query, preferred_element_type=jnp.float32) * head_width ** (-0.5)
    ).astype(jnp.bfloat16)
    queries = queries.reshape(row_count, col_count, HEADS, head_width)
    gate_act = jax.nn.sigmoid(jnp.dot(normed, w_gate, preferred_element_type=jnp.float32))

    def consume(running, segment, offset):
        run_max, run_sum, run_acc = running
        key_value = jnp.dot(segment, w_kv, preferred_element_type=jnp.float32).astype(jnp.bfloat16)
        tile_len = key_value.shape[1]
        key_tile = key_value[:, :, :chan_count].reshape(row_count, tile_len, HEADS, head_width)
        value_tile = key_value[:, :, chan_count:].reshape(row_count, tile_len, HEADS, head_width)
        scores = jnp.einsum(
            "rjhd,rkhd->rhjk", queries, key_tile, preferred_element_type=jnp.float32
        )
        bias_part = lax.dynamic_slice_in_dim(bias_query, offset, tile_len, 2).astype(jnp.float32)
        key_pos = offset + jnp.arange(tile_len, dtype=jnp.int32)
        key_mask = jnp.where(key_pos < key_limit, 0.0, -1000000000.0).astype(jnp.float32)
        scores = scores + bias_part[None] + key_mask
        new_max = jnp.maximum(run_max, jnp.max(scores, axis=-1))
        rescale = jnp.exp(run_max - new_max)
        expon = jnp.exp(scores - new_max[..., None])
        new_sum = run_sum * rescale + jnp.sum(expon, axis=-1)
        weights = expon.astype(jnp.bfloat16)
        partial_out = jnp.einsum(
            "rhjk,rkhd->rjhd", weights, value_tile, preferred_element_type=jnp.float32
        )
        new_acc = run_acc * jnp.transpose(rescale, (0, 2, 1))[..., None] + partial_out
        return (new_max, new_sum, new_acc)

    def fold_piece(running, segment, offset, project):
        tile_len = segment.shape[1]
        block_len = 512
        block_num = tile_len // block_len
        blocks = jnp.moveaxis(
            segment.reshape(row_count, block_num, block_len, segment.shape[2]), 1, 0
        )

        def advance(state_now, item_pair):
            block_tile, block_idx = item_pair
            return (consume(state_now, block_tile, block_idx * block_len), None)

        final_state, unused = lax.scan(
            advance, running, (blocks, jnp.arange(block_num, dtype=jnp.int32))
        )
        return final_state

    initial = (
        jnp.full((row_count, HEADS, col_count), -1e30, jnp.float32),
        jnp.zeros((row_count, HEADS, col_count), jnp.float32),
        jnp.zeros((row_count, col_count, HEADS, head_width), jnp.float32),
    )
    run_max, run_sum, run_acc = gather_keys(fold_piece, initial)
    attended = run_acc / jnp.transpose(run_sum, (0, 2, 1))[..., None]
    hidden = (gate_act * attended.reshape(row_count, col_count, chan_count)).astype(jnp.bfloat16)
    return jnp.dot(hidden, w_out, preferred_element_type=jnp.float32).astype(jnp.bfloat16)


def on_device(pair, w_query, w_kv, w_gate, w_out, pair_bias, lengths):
    key_limit = lengths[0]
    normed = normalize(pair)
    received = lax.all_to_all(pair_bias, "col", split_axis=2, concat_axis=1, tiled=True)
    bias_query = jnp.transpose(received, (0, 2, 1))

    def gather_keys(fold_piece, initial):
        return fold_piece(
            initial, lax.all_gather(normed, "col", axis=1, tiled=True), jnp.int32(0), True
        )

    return attend(normed, bias_query, key_limit, w_query, w_kv, w_gate, w_out, gather_keys)


def solution(mesh):
    in_specs = (P("grp", "col", None), P(), P(), P(), P(), P("grp", "col", None), P("grp"))
    out_specs = P("grp", "col", None)
    return jax.shard_map(
        on_device, mesh=mesh, in_specs=in_specs, out_specs=out_specs, check_vma=False
    )
```

profile of v0, /device:TPU:0, one launch (start us, length us, event | category | flops | bytes accessed | tf_op | source)
XLA Modules:
  0.0 114.1 jit_solution(4545162258831155141)
XLA Ops:
  6.5 1.1 convert_reduce_fusion
  7.6 1.2 %fusion.30 = f32[16,32]{1,0:T(8,128)S(1)} fusion(bf16[16,32,128]{2,1,0:T(8,128)(2,1)} %param.9, f32[16,32]{1,0:T(8,128)S(1)} %broadcast_multiply_fusion), kind=kLoop, calls=%fused_computation.40 | loop fusion | flops 261632 | bytes 135168 | tf_op jit(solution)/shard_map/reduce_sum | solution.py:13
  8.8 1.8 %fusion.31 = bf16[16,32,128]{2,1,0:T(8,128)(2,1)} fusion(bf16[16,32,128]{2,1,0:T(8,128)(2,1)} %param.9, f32[16,32]{1,0:T(8,128)S(1)} %add_rsqrt_fusion, f32[16,32]{1,0:T(8,128)S(1)} %broadcast_multiply_fusion), kind=kLoop, calls=%fused_computation.41 | loop fusion | flops 262144 | bytes 266240 | tf_op jit(solution)/shard_map/convert_element_type | solution.py:14
  10.6 1.6 %copy.17 = bf16[4,32,1024]{1,0,2:T(4,128)(2,1)S(1)} copy(bf16[4,32,1024]{2,1,0:T(8,128)(2,1)} %param.14) | data formatting | bytes 524288 | tf_op args[5]
  12.2 1.7 %reshape.48 = bf16[32,2,2048]{2,1,0:T(2,128)(2,1)} reshape(bf16[1024,4,32]{2,1,0:T(4,128)(2,1)S(1)} %bitcast.92) | data formatting | bytes 524288
  13.9 7.3 %all-to-all-start = ((bf16[32,2,2048]{2,1,0:T(2,128)(2,1)}), bf16[32,2,2048]{2,1,0:T(2,128)(2,1)S(1)}, u32[]{:S(2)}, u32[]{:S(2)}) async-start(bf16[32,2,2048]{2,1,0:T(2,128)(2,1)} %reshape.48), calls=%async_computation | async-start | bytes 524288 | tf_op jit(solution)/shard_map/all_to_all | solution.py:81
  21.3 1.1 fusion.27
  22.6 0.9 copy.21
  23.5 0.7 copy.20
  24.3 8.9 %all-to-all-done = bf16[32,2,2048]{2,1,0:T(2,128)(2,1)S(1)} async-done(((bf16[32,2,2048]{2,1,0:T(2,128)(2,1)}), bf16[32,2,2048]{2,1,0:T(2,128)(2,1)S(1)}, u32[]{:S(2)}, u32[]{:S(2)}) %all-to-all-start) | async-done | bytes 262176 | tf_op jit(solution)/shard_map/all_to_all | solution.py:81
  34.4 1.1 all_to_all.16
  35.5 42.7 %all-gather.2.cloned.1.call-done = bf16[16,1024,128]{2,1,0:T(8,128)(2,1)} async-done(((bf16[16,32,128]{2,1,0:T(8,128)(2,1)}), bf16[16,1024,128]{2,1,0:T(8,128)(2,1)}) %all-gather.2.cloned.1.call-update) | async-done | bytes 4194320 | tf_op jit(solution)/shard_map/all_gather | solution.py:86
  78.2 26.6 %while.15 = (s32[]{:T(128)}, f32[16,4,32]{2,1,0:T(4,128)S(1)}, f32[16,4,32]{2,1,0:T(4,128)S(1)}, f32[16,32,4,32]{1,3,2,0:T(8,128)S(1)}, bf16[2,16,512,128]{3,2,0...) while((s32[]{:T(128)}, f32[16,4,32]{2,1,0:T(4,128)S(1)}, ...), condition=%wide.region_5.6_spmd.clone, body=%wide.region_2.5_spmd.clone.sunk | while | flops 684996096 | bytes 52896580 | solution.py:62
  80.1 2.9 %convolution_convert_fusion.3 = bf16[16,512,256]{1,2,0:T(8,128)(2,1)S(1)} fusion(bf16[2,16,512,128]{3,2,0,1:T(8,128)(2,1)} %get-tuple-element.254, s32[]{:T(128)} %get-tuple-element.236, bf16[128,256]{0,1:T(8,128)(2,1)} %get-tuple-element.255), kind=kOutput, calls=%fused_computation.6.clone.1 | convolution fusion | flops 538968064 | bytes 6357504 | tf_op jit(solution)/shard_map/while/body/eval_jaxpr/dot_general | solution.py:28
  83.3 0.7 copy-done.2
  84.0 2.7 %fusion.65 = (f32[16,4,32]{2,1,0:T(4,128)S(1)}, f32[16,4,512,32]{2,3,1,0:T(8,128)}) fusion(f32[512]{0:T(512)S(1)} %fusion.63, f32[4,32,512]{2,1,0:T(8,128)S(1)} %dynamic-slice_convert_fusion.2, bf16[16,32,4,32]{3,1,2,0:T(8,128)(2,1)S(1)} %copy-done.2, bf16[16,512,4,32]{1,3,2,0:T(8,128)(2,1)S(1)} %bitcast.90), kind=kOutput, calls=%fused_computation.5.clone.1 | convolution fusion | flops 70252544 | bytes 6694912 | tf_op jit(solution)/shard_map/while/body/eval_jaxpr/rjhd,rkhd->rhjk/dot_general | solution.py:32
  86.8 3.4 %fusion.69 = f32[16,32,4,32]{1,3,2,0:T(8,128)S(1)} fusion(bf16[16,512,4,32]{1,3,2,0:T(8,128)(2,1)S(1)} %bitcast.89, f32[16,4,512,32]{2,3,1,0:T(8,128)} %get-tuple-element.219, f32[16,4,32]{2,1,0:T(4,128)S(1)} %get-tuple-element.251, f32[512]{0:T(512)S(1)} %fusion.63, f32[4,32,512]{2,1,0:T(8,128)S(1)} %dynamic-slice_convert_fusion.2, ...), kind=kOutput, calls=%fused_computation.14.clone.1 | convolution fusion | flops 71499776 | bytes 7096321 | tf_op jit(solution)/shard_map/while/body/eval_jaxpr/rhjk,rkhd->rjhd/dot_general | solution.py:44
  90.2 1.2 %fusion.67 = f32[16,4,32]{2,1,0:T(4,128)S(1)} fusion(f32[16,4,512,32]{2,3,1,0:T(8,128)S(1)} %copy-done.1, f32[16,4,32]{2,1,0:T(4,128)S(1)} %get-tuple-element.251, f32[512]{0:T(512)S(1)} %fusion.63, f32[4,32,512]{2,1,0:T(8,128)S(1)} %dynamic-slice_convert_fusion.2), kind=kLoop, calls=%fused_computation.4.clone.1 | loop fusion | flops 4192256 | bytes 4474880 | tf_op jit(solution)/shard_map/while/body/eval_jaxpr/reduce_sum | solution.py:42
  93.4 2.9 %convolution_convert_fusion.3 = bf16[16,512,256]{1,2,0:T(8,128)(2,1)S(1)} fusion(bf16[2,16,512,128]{3,2,0,1:T(8,128)(2,1)} %get-tuple-element.254, s32[]{:T(128)} %get-tuple-element.236, bf16[128,256]{0,1:T(8,128)(2,1)} %get-tuple-element.255), kind=kOutput, calls=%fused_computation.6.clone.1 | convolution fusion | flops 538968064 | bytes 6357504 | tf_op jit(solution)/shard_map/while/body/eval_jaxpr/dot_general | solution.py:28
  96.6 0.7 copy-done.2
  97.3 2.8 %fusion.65 = (f32[16,4,32]{2,1,0:T(4,128)S(1)}, f32[16,4,512,32]{2,3,1,0:T(8,128)}) fusion(f32[512]{0:T(512)S(1)} %fusion.63, f32[4,32,512]{2,1,0:T(8,128)S(1)} %dynamic-slice_convert_fusion.2, bf16[16,32,4,32]{3,1,2,0:T(8,128)(2,1)S(1)} %copy-done.2, bf16[16,512,4,32]{1,3,2,0:T(8,128)(2,1)S(1)} %bitcast.90), kind=kOutput, calls=%fused_computation.5.clone.1 | convolution fusion | flops 70252544 | bytes 6694912 | tf_op jit(solution)/shard_map/while/body/eval_jaxpr/rjhd,rkhd->rhjk/dot_general | solution.py:32
  100.1 3.4 %fusion.69 = f32[16,32,4,32]{1,3,2,0:T(8,128)S(1)} fusion(bf16[16,512,4,32]{1,3,2,0:T(8,128)(2,1)S(1)} %bitcast.89, f32[16,4,512,32]{2,3,1,0:T(8,128)} %get-tuple-element.219, f32[16,4,32]{2,1,0:T(4,128)S(1)} %get-tuple-element.251, f32[512]{0:T(512)S(1)} %fusion.63, f32[4,32,512]{2,1,0:T(8,128)S(1)} %dynamic-slice_convert_fusion.2, ...), kind=kOutput, calls=%fused_computation.14.clone.1 | convolution fusion | flops 71499776 | bytes 7096321 | tf_op jit(solution)/shard_map/while/body/eval_jaxpr/rhjk,rkhd->rjhd/dot_general | solution.py:44
  103.5 1.2 %fusion.67 = f32[16,4,32]{2,1,0:T(4,128)S(1)} fusion(f32[16,4,512,32]{2,3,1,0:T(8,128)S(1)} %copy-done.1, f32[16,4,32]{2,1,0:T(4,128)S(1)} %get-tuple-element.251, f32[512]{0:T(512)S(1)} %fusion.63, f32[4,32,512]{2,1,0:T(8,128)S(1)} %dynamic-slice_convert_fusion.2), kind=kLoop, calls=%fused_computation.4.clone.1 | loop fusion | flops 4192256 | bytes 4474880 | tf_op jit(solution)/shard_map/while/body/eval_jaxpr/reduce_sum | solution.py:42
  105.3 1.9 %convolution_convert_fusion.1 = bf16[16,32,128]{2,1,0:T(8,128)(2,1)} fusion(f32[16,32,128]{2,1,0:T(8,128)S(1)} %copy.23, bf16[16,32,128]{2,1,0:T(8,128)(2,1)} %fusion.31, bf16[128,128]{1,0:T(8,128)(2,1)} %param.13, bf16[128,128]{1,0:T(8,128)(2,1)} %param.12), kind=kOutput, calls=%fused_computation.34 | convolution fusion | flops 33947648 | bytes 589824 | tf_op jit(solution)/shard_map/dot_general | solution.py:75
  (45 shorter events, 5.3 us)
Async XLA Ops:
  6.5 14.7 %copy-start = (bf16[128,128]{1,0:T(8,128)(2,1)S(1)}, bf16[128,128]{1,0:T(8,128)(2,1)}, u32[]{:S(2)}) copy-start(bf16[128,128]{1,0:T(8,128)(2,1)} %param.10) | copy-start | bytes 98308
  6.5 17.0 %copy-start.5 = (bf16[128,256]{1,0:T(8,128)(2,1)S(1)}, bf16[128,256]{1,0:T(8,128)(2,1)}, u32[]{:S(2)}) copy-start(bf16[128,256]{1,0:T(8,128)(2,1)} %param.11) | copy-start | bytes 196612
  6.5 71.7 %all-gather.2.cloned.1.call-start = ((), (), s32[]{:S(2)}) async-start(), calls=%async_computation.1 | async-start | bytes 4325376 | tf_op jit(solution)/shard_map/all_gather | solution.py:86
  13.9 19.3 %all-to-all-start = ((bf16[32,2,2048]{2,1,0:T(2,128)(2,1)}), bf16[32,2,2048]{2,1,0:T(2,128)(2,1)S(1)}, u32[]{:S(2)}, u32[]{:S(2)}) async-start(bf16[32,2,2048]{2,1,0:T(2,128)(2,1)} %reshape.48), calls=%async_computation | async-start | bytes 524288 | tf_op jit(solution)/shard_map/all_to_all | solution.py:81
  78.2 1.9 %copy-start.3 = (bf16[4,32,1024]{2,1,0:T(8,128)(2,1)}, bf16[4,32,1024]{2,1,0:T(8,128)(2,1)S(1)}, u32[]{:S(2)}) copy-start(bf16[4,32,1024]{2,1,0:T(8,128)(2,1)S(1)} %get-tuple-element.258) | copy-start | bytes 786436 | tf_op jit(solution)/shard_map/while
  82.9 1.0 copy-start.2
  86.8 3.5 %copy-start.1 = (f32[16,4,512,32]{2,3,1,0:T(8,128)S(1)}, f32[16,4,512,32]{2,3,1,0:T(8,128)}, u32[]{:S(2)}) copy-start(f32[16,4,512,32]{2,3,1,0:T(8,128)} %get-tuple-element.219) | copy-start | bytes 12582916 | tf_op jit(solution)/shard_map/while
  90.2 1.3 %copy-start.4 = (bf16[4,32,1024]{2,1,0:T(8,128)(2,1)S(1)}, bf16[4,32,1024]{2,1,0:T(8,128)(2,1)}, u32[]{:S(2)}) copy-start(bf16[4,32,1024]{2,1,0:T(8,128)(2,1)} %copy-done.3) | copy-start | bytes 786436 | tf_op jit(solution)/shard_map/while
  91.5 1.9 %copy-start.3 = (bf16[4,32,1024]{2,1,0:T(8,128)(2,1)}, bf16[4,32,1024]{2,1,0:T(8,128)(2,1)S(1)}, u32[]{:S(2)}) copy-start(bf16[4,32,1024]{2,1,0:T(8,128)(2,1)S(1)} %get-tuple-element.258) | copy-start | bytes 786436 | tf_op jit(solution)/shard_map/while
  96.2 1.0 copy-start.2
  100.1 3.5 %copy-start.1 = (f32[16,4,512,32]{2,3,1,0:T(8,128)S(1)}, f32[16,4,512,32]{2,3,1,0:T(8,128)}, u32[]{:S(2)}) copy-start(f32[16,4,512,32]{2,3,1,0:T(8,128)} %get-tuple-element.219) | copy-start | bytes 12582916 | tf_op jit(solution)/shard_map/while
  103.5 1.3 %copy-start.4 = (bf16[4,32,1024]{2,1,0:T(8,128)(2,1)S(1)}, bf16[4,32,1024]{2,1,0:T(8,128)(2,1)}, u32[]{:S(2)}) copy-start(bf16[4,32,1024]{2,1,0:T(8,128)(2,1)} %copy-done.3) | copy-start | bytes 786436 | tf_op jit(solution)/shard_map/while
Sparse Core Ops, SparseCore 0:
  10.7 67.4 all-gather.1
where the time goes:
time: 115 us; the launch traced here: 114 us
  waiting for transfers between devices  51.7 us (45%)
  matrix products  21.1 us (18%)
  between operations  13.5 us (12%)
  local copies, waits for them, and re-layouts  11.1 us (10%)
  other arithmetic  8.07 us (7%)
  starting transfers between devices  7.33 us (6%)
  loops' own time  1.32 us (1%)
    all_gather x1, waiting for transfers between devices, gather_keys(): lax.all_gather(normed, 'col', axis=1, tiled=True)  42.7 us
    all_to_all x1, waiting for transfers between devices, on_device(): lax.all_to_all(pair_bias, 'col', split_axis=2, concat_axis=1, tiled=True)  8.93 us
    all_to_all x1, starting transfers between devices, on_device(): lax.all_to_all(pair_bias, 'col', split_axis=2, concat_axis=1, tiled=True)  7.33 us
    dot_general x2, matrix products, consume(): jnp.einsum('rhjk,rkhd->rjhd', weights, value_tile, preferred_element_type...  6.85 us
    dot_general x2, matrix products, consume(): jnp.dot(segment, w_kv, preferred_element_type=jnp.float32)  5.72 us
    dot_general x2, matrix products, consume(): jnp.einsum('rjhd,rkhd->rhjk', queries, key_tile, preferred_element_type=j...  5.51 us
    unnamed x9, local copies, waits for them, and re-layouts  5.47 us
    reduce_sum x2, other arithmetic, consume(): new_sum = run_sum * rescale + jnp.sum(expon, axis=-1)  2.38 us
  transfers between devices with their start and end apart: 2, of which 2 were waited for; matrix products, arithmetic and copies ran while one was open for 7% of the time, Pallas kernels for 0%

commit v1 on v0

--- a/solution.py
+++ b/solution.py
@@ -83,7 +83,12 @@
 
     def gather_keys(fold_piece, initial):
         return fold_piece(
-            initial, lax.all_gather(normed, "col", axis=1, tiled=True), jnp.int32(0), True
+            initial,
+            jnp.concatenate(
+                lax.all_to_all(jnp.stack([normed] * lax.axis_size("col")), "col", 0, 0), axis=1
+            ),
+            jnp.int32(0),
+            True,
         )
 
     return attend(normed, bias_query, key_limit, w_query, w_kv, w_gate, w_out, gather_keys)

time: 115 us -> 157 us (1.37)
  waiting for transfers between devices: 51.7 us -> 96.6 us
  between operations: 13.5 us -> 0.17 us
  local copies, waits for them, and re-layouts: 11.1 us -> 19.3 us
  starting transfers between devices: 7.33 us -> 11 us
    all_to_all x0 -> x1, waiting for transfers between devices: none -> 89.4 us  [gather_keys(): lax.all_to_all(jnp.stack([normed] * lax.axis_size('col')), 'col', 0, 0)]
    all_gather x1 -> x0, waiting for transfers between devices: 42.7 us -> none  [gather_keys(): lax.all_gather(normed, 'col', axis=1, tiled=True)]
    all_to_all x0 -> x1, local copies, waits for them, and re-layouts: none -> 5.22 us  [gather_keys(): lax.all_to_all(jnp.stack([normed] * lax.axis_size('col')), 'col', 0, 0)]
    all_to_all x0 -> x1, starting transfers between devices: none -> 3.69 us  [gather_keys(): lax.all_to_all(jnp.stack([normed] * lax.axis_size('col')), 'col', 0, 0)]
    another operation x0 -> x1, local copies, waits for them, and re-layouts: none -> 2.88 us  [gather_keys(): jnp.stack([normed] * lax.axis_size('col'))]
    all_to_all x1, waiting for transfers between devices: 8.93 us -> 7.21 us  [on_device(): lax.all_to_all(pair_bias, 'col', split_axis=2, concat_axis=1, tiled=True)]
    unnamed x9 -> x13, local copies, waits for them, and re-layouts: 5.47 us -> 5.47 us
  transfers between devices with their start and end apart: 2 -> 2, of which waited for: 2 -> 2; matrix products, arithmetic and copies ran while one was open for 7% -> 4% of each run, Pallas kernels for 0% -> 0%
where the time goes in v1:
time: 157 us; the launch traced here: 156 us
  waiting for transfers between devices  96.6 us (62%)
  matrix products  20.2 us (13%)
  local copies, waits for them, and re-layouts  19.3 us (12%)
  starting transfers between devices  11 us (7%)
  other arithmetic  7.35 us (5%)
    all_to_all x1, waiting for transfers between devices, gather_keys(): lax.all_to_all(jnp.stack([normed] * lax.axis_size('col')), 'col', 0, 0)  89.4 us
    all_to_all x1, starting transfers between devices, on_device(): lax.all_to_all(pair_bias, 'col', split_axis=2, concat_axis=1, tiled=True)  7.33 us
    all_to_all x1, waiting for transfers between devices, on_device(): lax.all_to_all(pair_bias, 'col', split_axis=2, concat_axis=1, tiled=True)  7.21 us
    dot_general x2, matrix products, consume(): jnp.einsum('rhjk,rkhd->rjhd', weights, value_tile, preferred_element_type...  6.85 us
    dot_general x2, matrix products, consume(): jnp.dot(segment, w_kv, preferred_element_type=jnp.float32)  5.71 us
    dot_general x2, matrix products, consume(): jnp.einsum('rjhd,rkhd->rhjk', queries, key_tile, preferred_element_type=j...  5.56 us
    unnamed x13, local copies, waits for them, and re-layouts  5.47 us
    all_to_all x1, local copies, waits for them, and re-layouts, gather_keys(): lax.all_to_all(jnp.stack([normed] * lax.axis_size('col')), 'col', 0, 0)  5.22 us
  transfers between devices with their start and end apart: 2, of which 2 were waited for; matrix products, arithmetic and copies ran while one was open for 4% of the time, Pallas kernels for 0%

profile of v1, /device:TPU:0, one launch (start us, length us, event | category | flops | bytes accessed | tf_op | source)
XLA Modules:
  0.0 156.1 jit_solution(4968276400579263814)
XLA Ops:
  0.0 1.6 %copy.18 = bf16[4,32,1024]{1,0,2:T(4,128)(2,1)S(1)} copy(bf16[4,32,1024]{2,1,0:T(8,128)(2,1)} %param.14) | data formatting | bytes 524288 | tf_op args[5]
  1.6 1.7 %reshape.50 = bf16[32,2,2048]{2,1,0:T(2,128)(2,1)} reshape(bf16[1024,4,32]{2,1,0:T(4,128)(2,1)S(1)} %bitcast.94) | data formatting | bytes 524288
  3.3 7.3 %all-to-all-start.1 = ((bf16[32,2,2048]{2,1,0:T(2,128)(2,1)}), bf16[32,2,2048]{2,1,0:T(2,128)(2,1)S(1)}, u32[]{:S(2)}, u32[]{:S(2)}) async-start(bf16[32,2,2048]{2,1,0:T(2,128)(2,1)} %reshape.50), calls=%async_computation.1 | async-start | bytes 524288 | tf_op jit(solution)/shard_map/all_to_all | solution.py:81
  10.6 1.0 convert_reduce_fusion
  11.7 1.2 fusion.30
  12.9 1.1 fusion.31
  14.0 7.2 %all-to-all-done.1 = bf16[32,2,2048]{2,1,0:T(2,128)(2,1)S(1)} async-done(((bf16[32,2,2048]{2,1,0:T(2,128)(2,1)}), bf16[32,2,2048]{2,1,0:T(2,128)(2,1)S(1)}, u32[]{:S(2)}, u32[]{:S(2)}) %all-to-all-start.1) | async-done | bytes 262176 | tf_op jit(solution)/shard_map/all_to_all | solution.py:81
  21.2 2.9 %stack.2 = bf16[32,16,32,128]{3,2,1,0:T(8,128)(2,1)} broadcast(bf16[16,32,128]{2,1,0:T(8,128)(2,1)S(1)} %fusion.31), dimensions={1,2,3} | broadcast | bytes 4325376 | tf_op jit(solution)/shard_map/stack | solution.py:88
  24.1 3.7 %all-to-all-start = ((bf16[32,16,32,128]{3,2,1,0:T(8,128)(2,1)}), bf16[32,16,32,128]{3,2,1,0:T(8,128)(2,1)}, u32[]{:S(2)}, u32[]{:S(2)}) async-start(bf16[32,16,32,128]{3,2,1,0:T(8,128)(2,1)} %stack.2), calls=%async_computation | async-start | bytes 8388608 | tf_op jit(solution)/shard_map/all_to_all | solution.py:88
  28.2 0.9 copy.22
  29.2 0.7 copy.21
  31.1 1.1 all_to_all.20
  32.2 89.4 %all-to-all-done = bf16[32,16,32,128]{3,2,1,0:T(8,128)(2,1)} async-done(((bf16[32,16,32,128]{3,2,1,0:T(8,128)(2,1)}), bf16[32,16,32,128]{3,2,1,0:T(8,128)(2,1)}, u32[]{:S(2)}, u32[]{:S(2)}) %all-to-all-start) | async-done | bytes 4194336 | tf_op jit(solution)/shard_map/all_to_all | solution.py:88
  121.7 5.2 %copy.17 = bf16[32,16,32,128]{3,2,0,1:T(8,128)(2,1)} copy(bf16[32,16,32,128]{3,2,1,0:T(8,128)(2,1)} %all-to-all-done) | data formatting | bytes 8388608 | tf_op jit(solution)/shard_map/all_to_all | solution.py:88
  126.9 26.9 %while.15 = (s32[]{:T(128)}, f32[16,4,32]{2,1,0:T(4,128)S(1)}, f32[16,4,32]{2,1,0:T(4,128)S(1)}, f32[16,32,4,32]{1,3,2,0:T(8,128)S(1)}, bf16[2,16,512,128]{3,2,0...) while((s32[]{:T(128)}, f32[16,4,32]{2,1,0:T(4,128)S(1)}, ...), condition=%wide.region_5.6_spmd.clone, body=%wide.region_2.5_spmd.clone.sunk | while | flops 684996096 | bytes 53158760 | solution.py:62
  128.9 2.9 %convolution_convert_fusion.3 = bf16[16,512,256]{1,2,0:T(8,128)(2,1)S(1)} fusion(bf16[2,16,512,128]{3,2,0,1:T(8,128)(2,1)} %get-tuple-element.254, s32[]{:T(128)} %get-tuple-element.236, bf16[128,256]{0,1:T(8,128)(2,1)S(1)} %get-tuple-element.255), kind=kOutput, calls=%fused_computation.6.clone.1 | convolution fusion | flops 538968064 | bytes 6357504 | tf_op jit(solution)/shard_map/while/body/eval_jaxpr/dot_general | solution.py:28
  132.8 2.8 %fusion.65 = (f32[16,4,32]{2,1,0:T(4,128)S(1)}, f32[16,4,512,32]{2,3,1,0:T(8,128)}) fusion(f32[512]{0:T(512)S(1)} %fusion.63, f32[4,32,512]{2,1,0:T(8,128)S(1)} %dynamic-slice_convert_fusion.2, bf16[16,32,4,32]{3,1,2,0:T(8,128)(2,1)S(1)} %copy-done.2, bf16[16,512,4,32]{1,3,2,0:T(8,128)(2,1)S(1)} %bitcast.92), kind=kOutput, calls=%fused_computation.5.clone.1 | convolution fusion | flops 70252544 | bytes 6694912 | tf_op jit(solution)/shard_map/while/body/eval_jaxpr/rjhd,rkhd->rhjk/dot_general | solution.py:32
  135.6 3.4 %fusion.69 = f32[16,32,4,32]{1,3,2,0:T(8,128)S(1)} fusion(bf16[16,512,4,32]{1,3,2,0:T(8,128)(2,1)S(1)} %bitcast.91, f32[16,4,512,32]{2,3,1,0:T(8,128)} %get-tuple-element.219, f32[16,4,32]{2,1,0:T(4,128)S(1)} %get-tuple-element.251, f32[512]{0:T(512)S(1)} %fusion.63, f32[4,32,512]{2,1,0:T(8,128)S(1)} %dynamic-slice_convert_fusion.2, ...), kind=kOutput, calls=%fused_computation.14.clone.1 | convolution fusion | flops 71499776 | bytes 7096321 | tf_op jit(solution)/shard_map/while/body/eval_jaxpr/rhjk,rkhd->rjhd/dot_general | solution.py:44
  139.0 1.2 fusion.67
  142.3 2.9 %convolution_convert_fusion.3 = bf16[16,512,256]{1,2,0:T(8,128)(2,1)S(1)} fusion(bf16[2,16,512,128]{3,2,0,1:T(8,128)(2,1)} %get-tuple-element.254, s32[]{:T(128)} %get-tuple-element.236, bf16[128,256]{0,1:T(8,128)(2,1)S(1)} %get-tuple-element.255), kind=kOutput, calls=%fused_computation.6.clone.1 | convolution fusion | flops 538968064 | bytes 6357504 | tf_op jit(solution)/shard_map/while/body/eval_jaxpr/dot_general | solution.py:28
  146.2 2.8 %fusion.65 = (f32[16,4,32]{2,1,0:T(4,128)S(1)}, f32[16,4,512,32]{2,3,1,0:T(8,128)}) fusion(f32[512]{0:T(512)S(1)} %fusion.63, f32[4,32,512]{2,1,0:T(8,128)S(1)} %dynamic-slice_convert_fusion.2, bf16[16,32,4,32]{3,1,2,0:T(8,128)(2,1)S(1)} %copy-done.2, bf16[16,512,4,32]{1,3,2,0:T(8,128)(2,1)S(1)} %bitcast.92), kind=kOutput, calls=%fused_computation.5.clone.1 | convolution fusion | flops 70252544 | bytes 6694912 | tf_op jit(solution)/shard_map/while/body/eval_jaxpr/rjhd,rkhd->rhjk/dot_general | solution.py:32
  149.0 3.4 %fusion.69 = f32[16,32,4,32]{1,3,2,0:T(8,128)S(1)} fusion(bf16[16,512,4,32]{1,3,2,0:T(8,128)(2,1)S(1)} %bitcast.91, f32[16,4,512,32]{2,3,1,0:T(8,128)} %get-tuple-element.219, f32[16,4,32]{2,1,0:T(4,128)S(1)} %get-tuple-element.251, f32[512]{0:T(512)S(1)} %fusion.63, f32[4,32,512]{2,1,0:T(8,128)S(1)} %dynamic-slice_convert_fusion.2, ...), kind=kOutput, calls=%fused_computation.14.clone.1 | convolution fusion | flops 71499776 | bytes 7096321 | tf_op jit(solution)/shard_map/while/body/eval_jaxpr/rhjk,rkhd->rjhd/dot_general | solution.py:44
  152.5 1.2 fusion.67
  154.2 1.9 %convolution_convert_fusion.1 = bf16[16,32,128]{2,1,0:T(8,128)(2,1)} fusion(f32[16,32,128]{2,1,0:T(8,128)S(1)} %copy.24, bf16[16,32,128]{2,1,0:T(8,128)(2,1)} %copy-done.7, bf16[128,128]{1,0:T(8,128)(2,1)} %param.13, bf16[128,128]{1,0:T(8,128)(2,1)} %param.12), kind=kOutput, calls=%fused_computation.34 | convolution fusion | flops 33947648 | bytes 589824 | tf_op jit(solution)/shard_map/dot_general | solution.py:75
  (54 shorter events, 7.0 us)
Async XLA Ops:
  0.0 27.8 %copy-start = (bf16[128,128]{1,0:T(8,128)(2,1)S(1)}, bf16[128,128]{1,0:T(8,128)(2,1)}, u32[]{:S(2)}) copy-start(bf16[128,128]{1,0:T(8,128)(2,1)} %param.10) | copy-start | bytes 98308
  3.3 17.9 %all-to-all-start.1 = ((bf16[32,2,2048]{2,1,0:T(2,128)(2,1)}), bf16[32,2,2048]{2,1,0:T(2,128)(2,1)S(1)}, u32[]{:S(2)}, u32[]{:S(2)}) async-start(bf16[32,2,2048]{2,1,0:T(2,128)(2,1)} %reshape.50), calls=%async_computation.1 | async-start | bytes 524288 | tf_op jit(solution)/shard_map/all_to_all | solution.py:81
  14.0 13.8 %copy-start.7 = (bf16[16,32,128]{2,1,0:T(8,128)(2,1)}, bf16[16,32,128]{2,1,0:T(8,128)(2,1)S(1)}, u32[]{:S(2)}) copy-start(bf16[16,32,128]{2,1,0:T(8,128)(2,1)S(1)} %fusion.31) | copy-start | bytes 393220
  24.1 5.1 %copy-start.8 = (bf16[128,256]{1,0:T(8,128)(2,1)S(1)}, bf16[128,256]{1,0:T(8,128)(2,1)}, u32[]{:S(2)}) copy-start(bf16[128,256]{1,0:T(8,128)(2,1)} %param.11) | copy-start | bytes 196612
  24.1 97.6 %all-to-all-start = ((bf16[32,16,32,128]{3,2,1,0:T(8,128)(2,1)}), bf16[32,16,32,128]{3,2,1,0:T(8,128)(2,1)}, u32[]{:S(2)}, u32[]{:S(2)}) async-start(bf16[32,16,32,128]{3,2,1,0:T(8,128)(2,1)} %stack.2), calls=%async_computation | async-start | bytes 8388608 | tf_op jit(solution)/shard_map/all_to_all | solution.py:88
  32.2 94.7 %copy-start.5 = (bf16[128,256]{0,1:T(8,128)(2,1)S(1)}, bf16[128,256]{0,1:T(8,128)(2,1)}, u32[]{:S(2)}) copy-start(bf16[128,256]{0,1:T(8,128)(2,1)} %copy.21) | copy-start | bytes 196612
  126.9 2.0 %copy-start.3 = (bf16[4,32,1024]{2,1,0:T(8,128)(2,1)}, bf16[4,32,1024]{2,1,0:T(8,128)(2,1)S(1)}, u32[]{:S(2)}) copy-start(bf16[4,32,1024]{2,1,0:T(8,128)(2,1)S(1)} %get-tuple-element.258) | copy-start | bytes 786436 | tf_op jit(solution)/shard_map/while
  131.7 1.0 copy-start.2
  135.6 3.5 %copy-start.1 = (f32[16,4,512,32]{2,3,1,0:T(8,128)S(1)}, f32[16,4,512,32]{2,3,1,0:T(8,128)}, u32[]{:S(2)}) copy-start(f32[16,4,512,32]{2,3,1,0:T(8,128)} %get-tuple-element.219) | copy-start | bytes 12582916 | tf_op jit(solution)/shard_map/while
  139.0 1.3 copy-start.4
  139.0 1.3 copy-start.6
  140.3 2.0 %copy-start.3 = (bf16[4,32,1024]{2,1,0:T(8,128)(2,1)}, bf16[4,32,1024]{2,1,0:T(8,128)(2,1)S(1)}, u32[]{:S(2)}) copy-start(bf16[4,32,1024]{2,1,0:T(8,128)(2,1)S(1)} %get-tuple-element.258) | copy-start | bytes 786436 | tf_op jit(solution)/shard_map/while
  145.2 1.0 copy-start.2
  149.0 3.5 %copy-start.1 = (f32[16,4,512,32]{2,3,1,0:T(8,128)S(1)}, f32[16,4,512,32]{2,3,1,0:T(8,128)}, u32[]{:S(2)}) copy-start(f32[16,4,512,32]{2,3,1,0:T(8,128)} %get-tuple-element.219) | copy-start | bytes 12582916 | tf_op jit(solution)/shard_map/while
  152.5 1.3 copy-start.4
  152.5 1.3 copy-start.6
